TPU v7x, 32 devices: a whole 2x2x4 slice. The times are simulated.
32 devices in a mesh: ctx: 8 (over z, y), head: 4 (over x, core).
Axes of the slice: x: 2, y: 2, z: 4, core: 2. Of those that a mesh axis runs over, the one named last changes fastest.
Arguments:
- queries: bfloat16 [4096, 32, 128], P(('ctx', 'head')), may hold values from -6 to 6
- key_states: bfloat16 [4096, 4, 128], P(('ctx', 'head')), may hold values from -6 to 6
- value_states: bfloat16 [4096, 4, 128], P(('ctx', 'head')), may hold values from -6 to 6
- out_grad: bfloat16 [4096, 32, 128], P(('ctx', 'head')), may hold values from -6 to 6
- log_sums: float32 [32, 4096], P('head', 'ctx'), may hold values from 3 to 6
- row_deltas: float32 [32, 4096], P('head', 'ctx'), may hold values from -10 to 10
- block_pairs: int32 [64, 4], replicated, may hold values from 0 to 63, as said below
- pair_kinds: int32 [64, 4], replicated, may hold values from 0 to 2, as said below
Outputs:
- query_grad: bfloat16 [4096, 32, 128], P(('ctx', 'head'))
- key_grad: bfloat16 [4096, 4, 128], P(('ctx', 'head'))
- value_grad: bfloat16 [4096, 4, 128], P(('ctx', 'head'))
Inputs may be any that keep to these rules, and one draw needn't show every extreme that they name: `block_pairs`: row g lists the key blocks of query block g. Slot 0 names g itself, slot 1 names g - 1, slot 2 names key block 0; slots 3 and up name blocks of shards at least two shards before the shard of g, never of shard 0. The blocks of the live slots of a row are distinct and none is later than g; a slot of kind 0 names block 0. Counting shards of 8 consecutive query blocks, the query blocks of one shard name at most one key block held by any other single shard, and this is reached. `pair_kinds`: 1 marks a full block pair, 2 the pair of a block with itself, 0 an unused slot. Slot 0 is always 2 and no other slot is 2; slot 1 is 0 only for g = 0; slot 2 is 0 exactly for g < 2 and for the query blocks of the second shard.
All inputs are finite; a program needn't handle non-finite values.
Results may differ from a plain program's by a relative error of at most 0.0012.
The roundings to bfloat16 on the way count: a program that leaves them out, or rounds other values in their place, can miss the bound.
Values may be sent and summed in bfloat16 or wider, within the bound.
A program may use at most 64 MiB of HBM per device.

v0:
```python
from functools import partial

import jax
import jax.numpy as jnp
from jax import lax
from jax.sharding import PartitionSpec as P

BLOCK = 64


def partner(block, axis, distance):
    count = lax.axis_size(axis)
    route = []
    for low in range(count):
        high = low | 1 << distance
        if high != low and high < count:
            route += [(low, high), (high, low)]
    return lax.ppermute(block, axis, route)


def tile_terms(
    query_part, grad_part, log_part, delta_part, key_tile, value_tile, slot_kinds, causal, lead_axis
):
    query_form = lead_axis + "bgd"
    score_scale = key_tile.shape[-1] ** (-0.5)
    scores = (
        jnp.einsum(
            query_form + ",nkd->ngbk", query_part, key_tile, preferred_element_type=jnp.float32
        )
        * score_scale
    )
    weights = jnp.exp(scores - log_part[..., None])
    full_pair = (slot_kinds == 1)[:, None, None, None]
    diagonal_pair = (slot_kinds == 2)[:, None, None, None]
    weights = jnp.where(full_pair | diagonal_pair & causal, weights, 0.0)
    value_term = jnp.einsum(
        "ngbk," + query_form + "->nkd",
        weights.astype(jnp.bfloat16),
        grad_part,
        preferred_element_type=jnp.float32,
    )
    prob_grad = jnp.einsum(
        query_form + ",nkd->ngbk", grad_part, value_tile, preferred_element_type=jnp.float32
    )
    dscore = (weights * (prob_grad - delta_part[..., None])).astype(jnp.bfloat16)
    query_term = (
        jnp.einsum("ngbk,nkd->" + query_form, dscore, key_tile, preferred_element_type=jnp.float32)
        * score_scale
    )
    key_term = (
        jnp.einsum(
            "ngbk," + query_form + "->nkd", dscore, query_part, preferred_element_type=jnp.float32
        )
        * score_scale
    )
    return (query_term, key_term, value_term)


def block_step(pair_acc, column, kv_table, causal):
    query_part, grad_part, log_part, delta_part, slot_index, slot_kinds = column
    tile_pair = kv_table[slot_index]
    query_term, key_term, value_term = tile_terms(
        query_part,
        grad_part,
        log_part,
        delta_part,
        tile_pair[:, :, 0],
        tile_pair[:, :, 1],
        slot_kinds,
        causal,
        "",
    )
    pair_acc = pair_acc.at[slot_index].add(jnp.stack([key_term, value_term], axis=2))
    return (pair_acc, query_term)


def relabel(source, my_rank):
    lookup = jnp.bitwise_xor(jnp.arange(source.shape[0], dtype=jnp.int32), my_rank)
    return jnp.take(source, lookup, axis=0)


def cube_cast(source, my_rank, bit_count, carries_grads):
    buffer = relabel(source, my_rank)
    for bit_level in range(bit_count):
        stride = 1 << bit_level
        halves = buffer.reshape((buffer.shape[0] // (2 * stride), 2, stride) + buffer.shape[1:])
        if carries_grads:
            incoming = partner(halves[:, 1], "ctx", bit_level)
        else:
            incoming = partner(halves[:, 1], "ctx", bit_level)
        buffer = jnp.concatenate([halves[:, :1], incoming[:, None]], axis=1).reshape(buffer.shape)
    return relabel(buffer, my_rank)


def shards(
    queries, key_states, value_states, out_grad, log_sums, row_deltas, block_pairs, pair_kinds
):
    head_queries, head_grads, head_keys, head_values = (
        lax.all_to_all(queries, "head", split_axis=1, concat_axis=0, tiled=True),
        lax.all_to_all(out_grad, "head", split_axis=1, concat_axis=0, tiled=True),
        lax.all_to_all(key_states, "head", split_axis=1, concat_axis=0, tiled=True),
        lax.all_to_all(value_states, "head", split_axis=1, concat_axis=0, tiled=True),
    )
    token_rows, head_group, head_width = head_queries.shape
    blocks_here = token_rows // BLOCK
    shard_count = lax.axis_size("ctx")
    my_rank = lax.axis_index("ctx")
    query_blocks = head_queries.reshape(blocks_here, BLOCK, head_group, head_width)
    grad_blocks = head_grads.reshape(blocks_here, BLOCK, head_group, head_width)
    kv_local = jnp.concatenate([head_keys, head_values], axis=1).reshape(
        blocks_here, BLOCK, 2, head_width
    )
    log_blocks = log_sums.reshape(head_group, blocks_here, BLOCK).transpose(1, 0, 2)
    delta_blocks = row_deltas.reshape(head_group, blocks_here, BLOCK).transpose(1, 0, 2)
    causal = jnp.arange(BLOCK)[:, None] >= jnp.arange(BLOCK)[None, :]
    my_pairs = lax.dynamic_slice_in_dim(block_pairs, my_rank * blocks_here, blocks_here, 0)
    my_kinds = lax.dynamic_slice_in_dim(pair_kinds, my_rank * blocks_here, blocks_here, 0)
    pair_owner = my_pairs // blocks_here
    table_index = jnp.where(
        pair_owner == my_rank, my_pairs - my_rank * blocks_here, blocks_here + pair_owner
    )
    every_owner = block_pairs // blocks_here
    asking_shard = (jnp.arange(block_pairs.shape[0], dtype=jnp.int32) // blocks_here)[:, None]
    is_asked = (pair_kinds > 0) & (every_owner == my_rank) & (asking_shard != my_rank)
    local_id = jnp.where(is_asked, block_pairs - my_rank * blocks_here, -1)
    wanted = jnp.max(local_id.reshape(shard_count, -1), axis=1)
    outgoing = kv_local[jnp.maximum(wanted, 0)]
    pair_acc = jnp.zeros((blocks_here + shard_count, BLOCK, 2, head_width), jnp.float32)
    first_slot = 0
    arrived = cube_cast(outgoing, my_rank, shard_count.bit_length() - 1, False)
    kv_table = jnp.concatenate([kv_local, arrived], axis=0)
    pair_acc, query_sums = lax.scan(
        partial(block_step, kv_table=kv_table, causal=causal),
        pair_acc,
        (query_blocks, grad_blocks, log_blocks, delta_blocks, table_index, my_kinds),
    )
    remote_sums = pair_acc[blocks_here:]
    returned = cube_cast(remote_sums, my_rank, shard_count.bit_length() - 1, True)
    chosen = (wanted[:, None] == jnp.arange(blocks_here, dtype=jnp.int32)[None, :]).astype(
        jnp.float32
    )
    kv_sums = pair_acc[:blocks_here] + jnp.einsum(
        "rl,rbcd->lbcd", chosen, returned, precision=lax.Precision.HIGHEST
    )
    key_out = kv_sums[:, :, 0].reshape(token_rows, 1, head_width).astype(jnp.bfloat16)
    value_out = kv_sums[:, :, 1].reshape(token_rows, 1, head_width).astype(jnp.bfloat16)
    query_out = query_sums.reshape(token_rows, head_group, head_width).astype(jnp.bfloat16)
    return (
        lax.all_to_all(query_out, "head", split_axis=0, concat_axis=1, tiled=True),
        lax.all_to_all(key_out, "head", split_axis=0, concat_axis=1, tiled=True),
        lax.all_to_all(value_out, "head", split_axis=0, concat_axis=1, tiled=True),
    )


def solution(mesh):
    in_specs = (
        P(("ctx", "head"), None, None),
        P(("ctx", "head"), None, None),
        P(("ctx", "head"), None, None),
        P(("ctx", "head"), None, None),
        P("head", "ctx"),
        P("head", "ctx"),
        P(),
        P(),
    )
    out_specs = (
        P(("ctx", "head"), None, None),
        P(("ctx", "head"), None, None),
        P(("ctx", "head"), None, None),
    )
    return jax.shard_map(shards, mesh=mesh, in_specs=in_specs, out_specs=out_specs, check_vma=False)
```

profile of v0, /device:TPU:0, one launch (start us, length us, event | category | flops | bytes accessed | tf_op | source)
XLA Modules:
  0.0 158.2 jit_solution(15268661662404538808)
XLA Ops:
  2.2 4.4 %all-to-all-start = ((bf16[128,4,128]{2,0,1:T(8,128)(2,1)}), bf16[128,4,128]{2,0,1:T(8,128)(2,1)S(1)}, u32[]{:S(2)}, u32[]{:S(2)}) async-start(bf16[128,4,128]{2,0,1:T(8,128)(2,1)} %copy.82), calls=%async_computation | async-start | bytes 262144 | tf_op jit(solution)/shard_map/all_to_all | solution.py:101
  8.2 2.6 %copy.88 = bf16[128,32,128]{2,0,1:T(8,128)(2,1)} copy(bf16[128,32,128]{2,1,0:T(8,128)(2,1)} %param.14) | data formatting | bytes 2097152 | tf_op args[0]
  11.2 3.3 %all-to-all-start.1 = ((bf16[128,4,128]{2,0,1:T(8,128)(2,1)}), bf16[128,4,128]{2,0,1:T(8,128)(2,1)S(1)}, u32[]{:S(2)}, u32[]{:S(2)}) async-start(bf16[128,4,128]{2,0,1:T(8,128)(2,1)} %copy.83), calls=%async_computation.1 | async-start | bytes 262144 | tf_op jit(solution)/shard_map/all_to_all | solution.py:102
  14.5 4.6 %all-to-all-done.1 = bf16[128,4,128]{2,0,1:T(8,128)(2,1)S(1)} async-done(((bf16[128,4,128]{2,0,1:T(8,128)(2,1)}), bf16[128,4,128]{2,0,1:T(8,128)(2,1)S(1)}, u32[]{:S(2)}, u32[]{:S(2)}) %all-to-all-start.1) | async-done | bytes 131104 | tf_op jit(solution)/shard_map/all_to_all | solution.py:102
  19.1 3.5 %all-to-all-start.2 = ((bf16[128,32,128]{2,0,1:T(8,128)(2,1)}), bf16[128,32,128]{2,0,1:T(8,128)(2,1)S(1)}, u32[]{:S(2)}, u32[]{:S(2)}) async-start(bf16[128,32,128]{2,0,1:T(8,128)(2,1)} %copy.88), calls=%async_computation.2 | async-start | bytes 2097152 | tf_op jit(solution)/shard_map/all_to_all | solution.py:99
  24.0 2.1 %collective-permute-start = (bf16[4,1,64,2,128]{4,2,3,0,1:T(8,128)(2,1)S(1)}, bf16[4,1,64,2,128]{4,2,3,0,1:T(8,128)(2,1)S(1)}, u32[]{:S(2)}, u32[]{:S(2)}) collective-permute-start(bf16[4,1,64,2,128]{4,2,3,0,1:T(8,128)(2,1)S(1)} %get-tuple-element.165), channel_id=1, source_target_pairs={{0,4},{4,0},{8,12},{12,8},{16,20},{20,16},{24,28},{28,24},{1,5},{5... | collective-permute-start | bytes 393224 | tf_op jit(solution)/shard_map/ppermute | solution.py:18
  26.1 4.1 %collective-permute-done = bf16[4,1,64,2,128]{4,2,3,0,1:T(8,128)(2,1)S(1)} collective-permute-done((bf16[4,1,64,2,128]{4,2,3,0,1:T(8,128)(2,1)S(1)}, bf16[4,1,64,2,128]{4,2,3,0,1:T(8,128)(2,1)S(1)}, u32[]{:S(2)}, u32[]{:S(2)}) %collective-permute-start) | collective-permute-done | bytes 131104 | tf_op jit(solution)/shard_map/ppermute | solution.py:18
  30.3 1.9 %collective-permute-start.1 = (bf16[2,2,64,2,128]{4,2,3,0,1:T(8,128)(2,1)S(1)}, bf16[2,2,64,2,128]{4,2,3,0,1:T(8,128)(2,1)S(1)}, u32[]{:S(2)}, u32[]{:S(2)}) collective-permute-start(bf16[2,2,64,2,128]{4,2,3,0,1:T(8,128)(2,1)S(1)} %get-tuple-element.163), channel_id=1, source_target_pairs={{0,8},{8,0},{4,12},{12,4},{16,24},{24,16},{20,28},{28,20},{1,9},{9... | collective-permute-start | bytes 393224 | tf_op jit(solution)/shard_map/ppermute | solution.py:18
  37.0 3.5 %all-to-all-start.3 = ((bf16[128,32,128]{2,0,1:T(8,128)(2,1)}), bf16[128,32,128]{2,0,1:T(8,128)(2,1)S(1)}, u32[]{:S(2)}, u32[]{:S(2)}) async-start(bf16[128,32,128]{2,0,1:T(8,128)(2,1)} %copy.91), calls=%async_computation.3 | async-start | bytes 2097152 | tf_op jit(solution)/shard_map/all_to_all | solution.py:100
  40.6 3.2 %collective-permute-start.2 = (bf16[1,4,64,2,128]{4,2,3,1,0:T(8,128)(2,1)S(1)}, bf16[1,4,64,2,128]{4,2,3,1,0:T(8,128)(2,1)S(1)}, u32[]{:S(2)}, u32[]{:S(2)}) collective-permute-start(bf16[1,4,64,2,128]{4,2,3,1,0:T(8,128)(2,1)S(1)} %get-tuple-element.161), channel_id=1, source_target_pairs={{0,16},{16,0},{4,20},{20,4},{8,24},{24,8},{12,28},{28,12},{1,17},{... | collective-permute-start | bytes 393224 | tf_op jit(solution)/shard_map/ppermute | solution.py:18
  43.8 6.9 %collective-permute-done.2 = bf16[1,4,64,2,128]{4,2,3,1,0:T(8,128)(2,1)S(1)} collective-permute-done((bf16[1,4,64,2,128]{4,2,3,1,0:T(8,128)(2,1)S(1)}, bf16[1,4,64,2,128]{4,2,3,1,0:T(8,128)(2,1)S(1)}, u32[]{:S(2)}, u32[]{:S(2)}) %collective-permute-start.2) | collective-permute-done | bytes 131104 | tf_op jit(solution)/shard_map/ppermute | solution.py:18
  53.0 2.0 %all-to-all-done.3 = bf16[128,32,128]{2,0,1:T(8,128)(2,1)S(1)} async-done(((bf16[128,32,128]{2,0,1:T(8,128)(2,1)}), bf16[128,32,128]{2,0,1:T(8,128)(2,1)S(1)}, u32[]{:S(2)}, u32[]{:S(2)}) %all-to-all-start.3) | async-done | bytes 1048608 | tf_op jit(solution)/shard_map/all_to_all | solution.py:100
  56.7 47.3 %while.13 = (s32[]{:T(128)}, f32[16,64,2,128]{3,1,2,0:T(8,128)S(1)}, bf16[8,64,8,128]{3,2,1,0:T(8,128)(2,1)}, s32[8,4]{1,0:T(8,128)S(1)}, s32[8,4]{1,0:T(8,128)S...) while((s32[]{:T(128)}, ...), condition=%wide.region_4.6_spmd.clone, body=%wide.region_2.5_spmd.clone.sunk | while | flops 169022480 | bytes 7221997 | solution.py:132
  104.9 2.1 %collective-permute-start.3 = (f32[4,1,64,2,128]{4,2,3,0,1:T(8,128)S(1)}, f32[4,1,64,2,128]{4,2,3,0,1:T(8,128)S(1)}, u32[]{:S(2)}, u32[]{:S(2)}) collective-permute-start(f32[4,1,64,2,128]{4,2,3,0,1:T(8,128)S(1)} %get-tuple-element.157), channel_id=1, source_target_pairs={{0,4},{4,0},{8,12},{12,8},{16,20},{20,16},{24,28},{28,24},{1,5},{5... | collective-permute-start | bytes 786440 | tf_op jit(solution)/shard_map/ppermute | solution.py:18
  107.0 6.0 %collective-permute-done.3 = f32[4,1,64,2,128]{4,2,3,0,1:T(8,128)S(1)} collective-permute-done((f32[4,1,64,2,128]{4,2,3,0,1:T(8,128)S(1)}, f32[4,1,64,2,128]{4,2,3,0,1:T(8,128)S(1)}, u32[]{:S(2)}, u32[]{:S(2)}) %collective-permute-start.3) | collective-permute-done | bytes 262176 | tf_op jit(solution)/shard_map/ppermute | solution.py:18
  114.9 5.4 %collective-permute-done.4 = f32[2,2,64,2,128]{4,2,3,1,0:T(8,128)S(1)} collective-permute-done((f32[2,2,64,2,128]{4,2,3,1,0:T(8,128)S(1)}, f32[2,2,64,2,128]{4,2,3,1,0:T(8,128)S(1)}, u32[]{:S(2)}, u32[]{:S(2)}) %collective-permute-start.4) | collective-permute-done | bytes 262176 | tf_op jit(solution)/shard_map/ppermute | solution.py:18
  120.4 2.6 %collective-permute-start.5 = (f32[1,4,64,2,128]{4,2,3,1,0:T(8,128)S(1)}, f32[1,4,64,2,128]{4,2,3,1,0:T(8,128)S(1)}, u32[]{:S(2)}, u32[]{:S(2)}) collective-permute-start(f32[1,4,64,2,128]{4,2,3,1,0:T(8,128)S(1)} %get-tuple-element.153), channel_id=1, source_target_pairs={{0,16},{16,0},{4,20},{20,4},{8,24},{24,8},{12,28},{28,12},{1,17},{... | collective-permute-start | bytes 786440 | tf_op jit(solution)/shard_map/ppermute | solution.py:18
  123.6 3.5 %all-to-all-start.4 = ((bf16[512,8,128]{2,1,0:T(8,128)(2,1)}), bf16[512,8,128]{2,1,0:T(8,128)(2,1)S(1)}, u32[]{:S(2)}, u32[]{:S(2)}) async-start(bf16[512,8,128]{2,1,0:T(8,128)(2,1)} %bitcast.28), calls=%async_computation.4 | async-start | bytes 2097152 | tf_op jit(solution)/shard_map/all_to_all | solution.py:149
  127.1 6.2 %collective-permute-done.5 = f32[1,4,64,2,128]{4,2,3,1,0:T(8,128)S(1)} collective-permute-done((f32[1,4,64,2,128]{4,2,3,1,0:T(8,128)S(1)}, f32[1,4,64,2,128]{4,2,3,1,0:T(8,128)S(1)}, u32[]{:S(2)}, u32[]{:S(2)}) %collective-permute-start.5) | collective-permute-done | bytes 262176 | tf_op jit(solution)/shard_map/ppermute | solution.py:18
  136.7 4.9 %all-to-all-done.4 = bf16[512,8,128]{2,1,0:T(8,128)(2,1)S(1)} async-done(((bf16[512,8,128]{2,1,0:T(8,128)(2,1)}), bf16[512,8,128]{2,1,0:T(8,128)(2,1)S(1)}, u32[]{:S(2)}, u32[]{:S(2)}) %all-to-all-start.4) | async-done | bytes 1048608 | tf_op jit(solution)/shard_map/all_to_all | solution.py:149
  141.5 3.3 %all-to-all-start.5 = ((bf16[4,2,8192]{2,1,0:T(2,128)(2,1)}), bf16[4,2,8192]{2,1,0:T(2,128)(2,1)S(1)}, u32[]{:S(2)}, u32[]{:S(2)}) async-start(bf16[4,2,8192]{2,1,0:T(2,128)(2,1)} %reshape.255), calls=%async_computation.5 | async-start | bytes 262144 | tf_op jit(solution)/shard_map/all_to_all | solution.py:150
  146.2 3.2 %all-to-all-done.5 = bf16[4,2,8192]{2,1,0:T(2,128)(2,1)S(1)} async-done(((bf16[4,2,8192]{2,1,0:T(2,128)(2,1)}), bf16[4,2,8192]{2,1,0:T(2,128)(2,1)S(1)}, u32[]{:S(2)}, u32[]{:S(2)}) %all-to-all-start.5) | async-done | bytes 131104 | tf_op jit(solution)/shard_map/all_to_all | solution.py:150
  149.4 3.3 %all-to-all-start.6 = ((bf16[4,2,8192]{2,1,0:T(2,128)(2,1)}), bf16[4,2,8192]{2,1,0:T(2,128)(2,1)S(1)}, u32[]{:S(2)}, u32[]{:S(2)}) async-start(bf16[4,2,8192]{2,1,0:T(2,128)(2,1)} %reshape.257), calls=%async_computation.6 | async-start | bytes 262144 | tf_op jit(solution)/shard_map/all_to_all | solution.py:151
  154.8 2.5 %all-to-all-done.6 = bf16[4,2,8192]{2,1,0:T(2,128)(2,1)S(1)} async-done(((bf16[4,2,8192]{2,1,0:T(2,128)(2,1)}), bf16[4,2,8192]{2,1,0:T(2,128)(2,1)S(1)}, u32[]{:S(2)}, u32[]{:S(2)}) %all-to-all-start.6) | async-done | bytes 131104 | tf_op jit(solution)/shard_map/all_to_all | solution.py:151
  (216 shorter events, 71.4 us)
Async XLA Ops:
  2.2 5.3 %copy-start.1 = (bf16[128,4,128]{2,1,0:T(4,128)(2,1)S(1)}, bf16[128,4,128]{2,1,0:T(4,128)(2,1)}, u32[]{:S(2)}) copy-start(bf16[128,4,128]{2,1,0:T(4,128)(2,1)} %param.16) | copy-start | bytes 393220
  2.2 9.0 %all-to-all-start = ((bf16[128,4,128]{2,0,1:T(8,128)(2,1)}), bf16[128,4,128]{2,0,1:T(8,128)(2,1)S(1)}, u32[]{:S(2)}, u32[]{:S(2)}) async-start(bf16[128,4,128]{2,0,1:T(8,128)(2,1)} %copy.82), calls=%async_computation | async-start | bytes 262144 | tf_op jit(solution)/shard_map/all_to_all | solution.py:101
  6.6 0.7 copy-start.5
  6.6 0.7 copy-start.4
  11.2 7.9 %all-to-all-start.1 = ((bf16[128,4,128]{2,0,1:T(8,128)(2,1)}), bf16[128,4,128]{2,0,1:T(8,128)(2,1)S(1)}, u32[]{:S(2)}, u32[]{:S(2)}) async-start(bf16[128,4,128]{2,0,1:T(8,128)(2,1)} %copy.83), calls=%async_computation.1 | async-start | bytes 262144 | tf_op jit(solution)/shard_map/all_to_all | solution.py:102
  19.1 17.9 %all-to-all-start.2 = ((bf16[128,32,128]{2,0,1:T(8,128)(2,1)}), bf16[128,32,128]{2,0,1:T(8,128)(2,1)S(1)}, u32[]{:S(2)}, u32[]{:S(2)}) async-start(bf16[128,32,128]{2,0,1:T(8,128)(2,1)} %copy.88), calls=%async_computation.2 | async-start | bytes 2097152 | tf_op jit(solution)/shard_map/all_to_all | solution.py:99
  23.2 9.2 %copy-start = (bf16[128,32,128]{2,1,0:T(8,128)(2,1)S(1)}, bf16[128,32,128]{2,1,0:T(8,128)(2,1)}, u32[]{:S(2)}) copy-start(bf16[128,32,128]{2,1,0:T(8,128)(2,1)} %param.17) | copy-start | bytes 3145732
  24.0 6.2 %collective-permute-start = (bf16[4,1,64,2,128]{4,2,3,0,1:T(8,128)(2,1)S(1)}, bf16[4,1,64,2,128]{4,2,3,0,1:T(8,128)(2,1)S(1)}, u32[]{:S(2)}, u32[]{:S(2)}) collective-permute-start(bf16[4,1,64,2,128]{4,2,3,0,1:T(8,128)(2,1)S(1)} %get-tuple-element.165), channel_id=1, source_target_pairs={{0,4},{4,0},{8,12},{12,8},{16,20},{20,16},{24,28},{28,24},{1,5},{5... | collective-permute-start | bytes 393224 | tf_op jit(solution)/shard_map/ppermute | solution.py:18
  30.3 5.4 %collective-permute-start.1 = (bf16[2,2,64,2,128]{4,2,3,0,1:T(8,128)(2,1)S(1)}, bf16[2,2,64,2,128]{4,2,3,0,1:T(8,128)(2,1)S(1)}, u32[]{:S(2)}, u32[]{:S(2)}) collective-permute-start(bf16[2,2,64,2,128]{4,2,3,0,1:T(8,128)(2,1)S(1)} %get-tuple-element.163), channel_id=1, source_target_pairs={{0,8},{8,0},{4,12},{12,4},{16,24},{24,16},{20,28},{28,20},{1,9},{9... | collective-permute-start | bytes 393224 | tf_op jit(solution)/shard_map/ppermute | solution.py:18
  32.4 1.4 copy-start.2
  33.9 0.7 copy-start.3
  37.0 17.9 %all-to-all-start.3 = ((bf16[128,32,128]{2,0,1:T(8,128)(2,1)}), bf16[128,32,128]{2,0,1:T(8,128)(2,1)S(1)}, u32[]{:S(2)}, u32[]{:S(2)}) async-start(bf16[128,32,128]{2,0,1:T(8,128)(2,1)} %copy.91), calls=%async_computation.3 | async-start | bytes 2097152 | tf_op jit(solution)/shard_map/all_to_all | solution.py:100
  40.6 10.1 %collective-permute-start.2 = (bf16[1,4,64,2,128]{4,2,3,1,0:T(8,128)(2,1)S(1)}, bf16[1,4,64,2,128]{4,2,3,1,0:T(8,128)(2,1)S(1)}, u32[]{:S(2)}, u32[]{:S(2)}) collective-permute-start(bf16[1,4,64,2,128]{4,2,3,1,0:T(8,128)(2,1)S(1)} %get-tuple-element.161), channel_id=1, source_target_pairs={{0,16},{16,0},{4,20},{20,4},{8,24},{24,8},{12,28},{28,12},{1,17},{... | collective-permute-start | bytes 393224 | tf_op jit(solution)/shard_map/ppermute | solution.py:18
  104.9 8.1 %collective-permute-start.3 = (f32[4,1,64,2,128]{4,2,3,0,1:T(8,128)S(1)}, f32[4,1,64,2,128]{4,2,3,0,1:T(8,128)S(1)}, u32[]{:S(2)}, u32[]{:S(2)}) collective-permute-start(f32[4,1,64,2,128]{4,2,3,0,1:T(8,128)S(1)} %get-tuple-element.157), channel_id=1, source_target_pairs={{0,4},{4,0},{8,12},{12,8},{16,20},{20,16},{24,28},{28,24},{1,5},{5... | collective-permute-start | bytes 786440 | tf_op jit(solution)/shard_map/ppermute | solution.py:18
  113.1 7.2 %collective-permute-start.4 = (f32[2,2,64,2,128]{4,2,3,1,0:T(8,128)S(1)}, f32[2,2,64,2,128]{4,2,3,1,0:T(8,128)S(1)}, u32[]{:S(2)}, u32[]{:S(2)}) collective-permute-start(f32[2,2,64,2,128]{4,2,3,1,0:T(8,128)S(1)} %bitcast.237), channel_id=1, source_target_pairs={{0,8},{8,0},{4,12},{12,4},{16,24},{24,16},{20,28},{28,20},{1,9},{9... | collective-permute-start | bytes 786440 | tf_op jit(solution)/shard_map/ppermute | solution.py:18
  120.4 12.9 %collective-permute-start.5 = (f32[1,4,64,2,128]{4,2,3,1,0:T(8,128)S(1)}, f32[1,4,64,2,128]{4,2,3,1,0:T(8,128)S(1)}, u32[]{:S(2)}, u32[]{:S(2)}) collective-permute-start(f32[1,4,64,2,128]{4,2,3,1,0:T(8,128)S(1)} %get-tuple-element.153), channel_id=1, source_target_pairs={{0,16},{16,0},{4,20},{20,4},{8,24},{24,8},{12,28},{28,12},{1,17},{... | collective-permute-start | bytes 786440 | tf_op jit(solution)/shard_map/ppermute | solution.py:18
  123.6 17.9 %all-to-all-start.4 = ((bf16[512,8,128]{2,1,0:T(8,128)(2,1)}), bf16[512,8,128]{2,1,0:T(8,128)(2,1)S(1)}, u32[]{:S(2)}, u32[]{:S(2)}) async-start(bf16[512,8,128]{2,1,0:T(8,128)(2,1)} %bitcast.28), calls=%async_computation.4 | async-start | bytes 2097152 | tf_op jit(solution)/shard_map/all_to_all | solution.py:149
  141.5 7.9 %all-to-all-start.5 = ((bf16[4,2,8192]{2,1,0:T(2,128)(2,1)}), bf16[4,2,8192]{2,1,0:T(2,128)(2,1)S(1)}, u32[]{:S(2)}, u32[]{:S(2)}) async-start(bf16[4,2,8192]{2,1,0:T(2,128)(2,1)} %reshape.255), calls=%async_computation.5 | async-start | bytes 262144 | tf_op jit(solution)/shard_map/all_to_all | solution.py:150
  149.4 7.9 %all-to-all-start.6 = ((bf16[4,2,8192]{2,1,0:T(2,128)(2,1)}), bf16[4,2,8192]{2,1,0:T(2,128)(2,1)S(1)}, u32[]{:S(2)}, u32[]{:S(2)}) async-start(bf16[4,2,8192]{2,1,0:T(2,128)(2,1)} %reshape.257), calls=%async_computation.6 | async-start | bytes 262144 | tf_op jit(solution)/shard_map/all_to_all | solution.py:151
where the time goes:
time: 160 us; the launch traced here: 158 us
  waiting for transfers between devices  48.3 us (30%)
  local copies, waits for them, and re-layouts  45.9 us (29%)
  starting transfers between devices  38.6 us (24%)
  matrix products  13.4 us (8%)
  other arithmetic  10.2 us (6%)
    ppermute x6, waiting for transfers between devices, partner(): return lax.ppermute(block, axis, route)  29.6 us
    ppermute x6, starting transfers between devices, partner(): return lax.ppermute(block, axis, route)  13.7 us
    gather x8, local copies, waits for them, and re-layouts, block_step(): tile_pair = kv_table[slot_index]  12.9 us
    unnamed x28, local copies, waits for them, and re-layouts  11 us
    dynamic_slice x16, local copies, waits for them, and re-layouts, shards(): lax.scan(partial(block_step, kv_table=kv_table, causal=causal), pair_acc,...  7.55 us
    scatter-add x8, other arithmetic, block_step(): pair_acc.at[slot_index].add(jnp.stack([key_term, value_term], axis=2))  6.01 us
    dynamic_update_slice x8, local copies, waits for them, and re-layouts, shards(): lax.scan(partial(block_step, kv_table=kv_table, causal=causal), pair_acc,...  6 us
    all_to_all x1, waiting for transfers between devices, shards(): lax.all_to_all(query_out, 'head', split_axis=0, concat_axis=1, tiled=True)  4.85 us
  transfers between devices with their start and end apart: 13, of which 13 were waited for; matrix products, arithmetic and copies ran while one was open for 10% of the time, Pallas kernels for 0%

commit v1 on v0

v1 whole, which is shorter than its diff:
```python
from functools import partial

import jax
import jax.numpy as jnp
from jax import lax
from jax.experimental import pallas as pl
from jax.experimental.pallas import tpu as pltpu
from jax.sharding import PartitionSpec as P

BLOCK = 64
MESH = pl.DeviceIdType.MESH


def kernel(
    n_ctx,
    n_head,
    n_slot,
    pair_tab,
    kind_tab,
    q_hbm,
    g_hbm,
    kv_in,
    log_ref,
    delta_ref,
    dq_out,
    dkv_out,
    q_buf,
    g_buf,
    kv_loc,
    outgoing,
    arrived,
    kcat,
    log_rows,
    delta_rows,
    acc,
    acc_hub,
    far_terms,
    dq_buf,
    part,
    ret,
    fin,
    kv_send,
    kv_recv,
    q_send,
    q_recv,
    g_send,
    g_recv,
    arr_send,
    arr_recv,
    dq_send,
    dq_recv,
    ret_send,
    ret_recv,
    fin_send,
    fin_recv,
):
    rank = lax.axis_index("ctx")
    me = lax.axis_index("head")
    rows = q_hbm.shape[0]
    heads = q_hbm.shape[1] // n_head
    width = q_hbm.shape[2]
    per_src = rows // BLOCK
    blocks = per_src * n_head
    lanes = BLOCK * heads
    keys = n_slot * BLOCK
    scale = width ** (-0.5)

    def peer(d):
        return lax.rem(me // 2 + d // 2, n_head // 2) * 2 + lax.rem(
            lax.rem(me, 2) + lax.rem(d, 2), 2
        )

    barrier = pltpu.get_barrier_semaphore()
    for d in range(1, n_head):
        pl.semaphore_signal(barrier, inc=1, device_id=(rank, peer(d)), device_id_type=MESH)

    def greet(k, c):
        pl.semaphore_signal(
            barrier, inc=1, device_id=(lax.rem(rank + k, n_ctx), me), device_id_type=MESH
        )
        return c

    lax.fori_loop(1, n_ctx, greet, 0)
    pl.semaphore_wait(barrier, n_ctx + n_head - 2)

    def kv_copy(p):
        return pltpu.make_async_remote_copy(
            src_ref=kv_in.at[p],
            dst_ref=kv_loc.at[pl.ds(me * per_src, per_src)],
            send_sem=kv_send.at[p],
            recv_sem=kv_recv.at[me],
            device_id=(rank, p),
            device_id_type=MESH,
        )

    def token_copy(src, dst, send, recv, p, j):
        return pltpu.make_async_remote_copy(
            src_ref=src.at[pl.ds(j * BLOCK, BLOCK), pl.ds(pl.multiple_of(p * heads, heads), heads)],
            dst_ref=dst.at[me, j],
            send_sem=send.at[p, j],
            recv_sem=recv.at[me, j],
            device_id=(rank, p),
            device_id_type=MESH,
        )

    def own_copy(src, dst, recv, j):
        return pltpu.make_async_copy(
            src.at[pl.ds(j * BLOCK, BLOCK), pl.ds(pl.multiple_of(me * heads, heads), heads)],
            dst.at[me, j],
            recv.at[me, j],
        )

    far_first = list(range(2, n_head)) + [1]
    for d in far_first:
        kv_copy(peer(d)).start()
    own_kv = pltpu.make_async_copy(
        kv_in.at[me], kv_loc.at[pl.ds(me * per_src, per_src)], kv_recv.at[me]
    )
    own_kv.start()
    for j in range(per_src):
        own_copy(q_hbm, q_buf, q_recv, j).start()
        own_copy(g_hbm, g_buf, g_recv, j).start()
    for j in range(per_src):
        for d in far_first:
            token_copy(q_hbm, q_buf, q_send, q_recv, peer(d), j).start()
            token_copy(g_hbm, g_buf, g_send, g_recv, peer(d), j).start()

    spread = (
        lax.broadcasted_iota(jnp.int32, (BLOCK, lanes), 1) // heads
        == lax.broadcasted_iota(jnp.int32, (BLOCK, lanes), 0)
    ).astype(jnp.float32)
    own_row = lax.broadcasted_iota(jnp.int32, (heads, lanes), 1) % heads == lax.broadcasted_iota(
        jnp.int32, (heads, lanes), 0
    )
    for stat_ref, stat_rows in ((log_ref, log_rows), (delta_ref, delta_rows)):
        for i in range(blocks):
            wide = jnp.dot(
                stat_ref[:, i * BLOCK : (i + 1) * BLOCK],
                spread,
                precision=lax.Precision.HIGHEST,
                preferred_element_type=jnp.float32,
            )
            stat_rows[i] = jnp.sum(jnp.where(own_row, wide, 0.0), axis=0, keepdims=True)
    acc[...] = jnp.zeros_like(acc)
    acc_hub[...] = jnp.zeros_like(acc_hub)

    own_kv.wait()
    for d in range(1, n_head):
        p = peer(d)
        kv_here = kv_loc.at[pl.ds(p * per_src, per_src)]
        pltpu.make_async_copy(kv_here, kv_here, kv_recv.at[p]).wait()

    first = rank * blocks

    def wanted_by(s):
        best = jnp.where(rank + 1 == s, blocks - 1, 0)
        for i in range(blocks):
            at = s * blocks + i
            for j in range(3, n_slot):
                local = pair_tab[j, at] - first
                named = (kind_tab[j, at] > 0) & (local >= 0) & (local < blocks)
                best = jnp.where(named, jnp.maximum(best, local), best)
        return best

    def arr_copy(s):
        return pltpu.make_async_remote_copy(
            src_ref=outgoing.at[s],
            dst_ref=arrived.at[rank],
            send_sem=arr_send.at[s],
            recv_sem=arr_recv.at[rank],
            device_id=(s, me),
            device_id_type=MESH,
        )

    def send_block(s, c):
        outgoing[s] = kv_loc[wanted_by(s)]
        arr_copy(s).start()
        return c

    lax.fori_loop(rank + 1, n_ctx, send_block, 0)
    arrived[rank] = kv_loc[0]

    def take_block(o, c):
        pltpu.make_async_copy(arrived.at[o], arrived.at[o], arr_recv.at[o]).wait()
        return c

    lax.fori_loop(0, rank, take_block, 0)

    key_row = lax.broadcasted_iota(jnp.int32, (keys, lanes), 0)
    causal = (key_row >= BLOCK) | (
        key_row <= lax.broadcasted_iota(jnp.int32, (keys, lanes), 1) // heads
    )

    def dq_copy(p, j):
        return pltpu.make_async_remote_copy(
            src_ref=dq_buf.at[p, j],
            dst_ref=dq_out.at[
                pl.ds(j * BLOCK, BLOCK), pl.ds(pl.multiple_of(me * heads, heads), heads)
            ],
            send_sem=dq_send.at[p, j],
            recv_sem=dq_recv.at[me, j],
            device_id=(rank, p),
            device_id_type=MESH,
        )

    def own_dq(j):
        return pltpu.make_async_copy(
            dq_buf.at[me, j],
            dq_out.at[pl.ds(j * BLOCK, BLOCK), pl.ds(pl.multiple_of(me * heads, heads), heads)],
            dq_recv.at[me, j],
        )

    def far_owner(i, j):
        at = first + i
        return jnp.where(kind_tab[j, at] > 0, lax.div(pair_tab[j, at], blocks), rank)

    def block_step(t, c):
        d = t // per_src
        j = lax.rem(t, per_src)
        p = peer(d)
        i = p * per_src + j
        pltpu.make_async_copy(q_buf.at[p, j], q_buf.at[p, j], q_recv.at[p, j]).wait()
        pltpu.make_async_copy(g_buf.at[p, j], g_buf.at[p, j], g_recv.at[p, j]).wait()
        kcat[0:BLOCK] = kv_loc[i]
        kcat[BLOCK : 2 * BLOCK] = jnp.where(
            i == 0,
            arrived[jnp.maximum(rank - 1, 0)],
            kv_loc[jnp.maximum(i - 1, 0)],
        )
        kcat[2 * BLOCK : 3 * BLOCK] = arrived[0]
        for slot in range(3, n_slot):
            kcat[slot * BLOCK : (slot + 1) * BLOCK] = arrived[far_owner(i, slot)]
        key_tile = kcat[:, :width]
        value_tile = kcat[:, width:]
        q = q_buf[p, j].astype(jnp.float32).reshape(lanes, width).astype(jnp.bfloat16)
        g = g_buf[p, j].astype(jnp.float32).reshape(lanes, width).astype(jnp.bfloat16)
        nt = (((1,), (1,)), ((), ()))
        scores = lax.dot_general(key_tile, q, nt, preferred_element_type=jnp.float32) * scale
        weights = jnp.exp(scores - log_rows[i])
        slot_mask = jnp.ones((keys, 1), jnp.int32)
        slot_row = lax.broadcasted_iota(jnp.int32, (keys, 1), 0) // BLOCK
        for slot in range(1, n_slot):
            kind = kind_tab[slot, first + i]
            slot_mask = jnp.where(slot_row == slot, kind, slot_mask)
        weights = jnp.where(causal & (slot_mask > 0), weights, 0.0)
        rounded = weights.astype(jnp.bfloat16)
        prob_grad = lax.dot_general(value_tile, g, nt, preferred_element_type=jnp.float32)
        dscore = (weights * (prob_grad - delta_rows[i])).astype(jnp.bfloat16)
        dv = jnp.dot(rounded, g, preferred_element_type=jnp.float32)
        dk = jnp.dot(dscore, q, preferred_element_type=jnp.float32)
        dq = lax.dot_general(
            dscore, key_tile, (((0,), (0,)), ((), ())), preferred_element_type=jnp.float32
        )
        dq_buf[p, j] = (dq * scale).reshape(BLOCK, heads, width).astype(jnp.bfloat16)

        @pl.when(d == 0)
        def _():
            own_dq(j).start()

        @pl.when(d > 0)
        def _():
            dq_copy(p, j).start()

        acc[i + 1, :, :width] += dk[:BLOCK]
        acc[i + 1, :, width:] += dv[:BLOCK]
        acc[i, :, :width] += dk[BLOCK : 2 * BLOCK]
        acc[i, :, width:] += dv[BLOCK : 2 * BLOCK]
        acc_hub[:, :width] += dk[2 * BLOCK : 3 * BLOCK]
        acc_hub[:, width:] += dv[2 * BLOCK : 3 * BLOCK]
        for slot in range(3, n_slot):
            far_terms[i, slot - 3, :, :width] = dk[slot * BLOCK : (slot + 1) * BLOCK]
            far_terms[i, slot - 3, :, width:] = dv[slot * BLOCK : (slot + 1) * BLOCK]
        return c

    lax.fori_loop(0, blocks, block_step, 0)

    def ret_copy(o):
        return pltpu.make_async_remote_copy(
            src_ref=part.at[o],
            dst_ref=ret.at[rank],
            send_sem=ret_send.at[o],
            recv_sem=ret_recv.at[rank],
            device_id=(o, me),
            device_id_type=MESH,
        )

    def send_part(o, c):
        terms = jnp.where(o == 0, acc_hub[...], 0.0) + jnp.where(o == rank - 1, acc[0], 0.0)
        for i in range(blocks):
            for slot in range(3, n_slot):
                terms += jnp.where(far_owner(i, slot) == o, far_terms[i, slot - 3], 0.0)
        part[o] = terms
        ret_copy(o).start()
        return c

    lax.fori_loop(0, rank, send_part, 0)

    acc[1] += jnp.where(rank == 0, acc_hub[...], 0.0)

    def take_part(s, c):
        pltpu.make_async_copy(ret.at[s], ret.at[s], ret_recv.at[s]).wait()
        b = wanted_by(s)
        for i in range(blocks):
            acc[i + 1] += jnp.where(b == i, ret[s], 0.0)
        return c

    lax.fori_loop(rank + 1, n_ctx, take_part, 0)

    for i in range(blocks):
        j = i % per_src
        fin[i // per_src, j, :, :width] = (acc[i + 1, :, :width] * scale).astype(jnp.bfloat16)
        fin[i // per_src, j, :, width:] = acc[i + 1, :, width:].astype(jnp.bfloat16)

    def fin_copy(p):
        return pltpu.make_async_remote_copy(
            src_ref=fin.at[p],
            dst_ref=dkv_out.at[me],
            send_sem=fin_send.at[p],
            recv_sem=fin_recv.at[me],
            device_id=(rank, p),
            device_id_type=MESH,
        )

    for d in far_first:
        fin_copy(peer(d)).start()
    own_fin = pltpu.make_async_copy(fin.at[me], dkv_out.at[me], fin_recv.at[me])
    own_fin.start()

    def sent_block(s, c):
        arr_copy(s).wait_send()
        return c

    lax.fori_loop(rank + 1, n_ctx, sent_block, 0)

    def sent_part(o, c):
        ret_copy(o).wait_send()
        return c

    lax.fori_loop(0, rank, sent_part, 0)
    for d in range(1, n_head):
        p = peer(d)
        kv_copy(p).wait_send()
        for j in range(per_src):
            token_copy(q_hbm, q_buf, q_send, q_recv, p, j).wait_send()
            token_copy(g_hbm, g_buf, g_send, g_recv, p, j).wait_send()
            dq_copy(p, j).wait_send()
            dq_here = dq_out.at[
                pl.ds(j * BLOCK, BLOCK), pl.ds(pl.multiple_of(p * heads, heads), heads)
            ]
            pltpu.make_async_copy(dq_here, dq_here, dq_recv.at[p, j]).wait()
        fin_copy(p).wait_send()
        pltpu.make_async_copy(dkv_out.at[p], dkv_out.at[p], fin_recv.at[p]).wait()
    for j in range(per_src):
        own_dq(j).wait()
    own_fin.wait()


def shards(
    n_ctx,
    n_head,
    queries,
    key_states,
    value_states,
    out_grad,
    log_sums,
    row_deltas,
    block_pairs,
    pair_kinds,
):
    rows, all_heads, width = queries.shape
    heads = all_heads // n_head
    n_slot = block_pairs.shape[1]
    per_src = rows // BLOCK
    blocks = per_src * n_head
    lanes = BLOCK * heads
    bf16, f32 = jnp.bfloat16, jnp.float32
    kv = jnp.concatenate([key_states, value_states], axis=-1).transpose(1, 0, 2)
    kv = kv.reshape(n_head, per_src, BLOCK, 2 * width)
    vmem = pl.BlockSpec(memory_space=pltpu.VMEM)
    anywhere = pl.BlockSpec(memory_space=pl.ANY)
    dma = pltpu.SemaphoreType.DMA
    dq, dkv = pl.pallas_call(
        partial(kernel, n_ctx, n_head, n_slot),
        out_shape=(
            jax.ShapeDtypeStruct(queries.shape, bf16),
            jax.ShapeDtypeStruct(kv.shape, bf16),
        ),
        in_specs=[
            pl.BlockSpec(memory_space=pltpu.SMEM),
            pl.BlockSpec(memory_space=pltpu.SMEM),
            anywhere,
            anywhere,
            vmem,
            vmem,
            vmem,
        ],
        out_specs=(anywhere, vmem),
        scratch_shapes=[
            pltpu.VMEM((n_head, per_src, BLOCK, heads, width), bf16),
            pltpu.VMEM((n_head, per_src, BLOCK, heads, width), bf16),
            pltpu.VMEM((blocks, BLOCK, 2 * width), bf16),
            pltpu.VMEM((n_ctx, BLOCK, 2 * width), bf16),
            pltpu.VMEM((n_ctx, BLOCK, 2 * width), bf16),
            pltpu.VMEM((n_slot * BLOCK, 2 * width), bf16),
            pltpu.VMEM((blocks, 1, lanes), f32),
            pltpu.VMEM((blocks, 1, lanes), f32),
            pltpu.VMEM((blocks + 1, BLOCK, 2 * width), f32),
            pltpu.VMEM((BLOCK, 2 * width), f32),
            pltpu.VMEM((blocks, n_slot - 3, BLOCK, 2 * width), f32),
            pltpu.VMEM((n_head, per_src, BLOCK, heads, width), bf16),
            pltpu.VMEM((n_ctx, BLOCK, 2 * width), f32),
            pltpu.VMEM((n_ctx, BLOCK, 2 * width), f32),
            pltpu.VMEM((n_head, per_src, BLOCK, 2 * width), bf16),
            dma((n_head,)),
            dma((n_head,)),
            dma((n_head, per_src)),
            dma((n_head, per_src)),
            dma((n_head, per_src)),
            dma((n_head, per_src)),
            dma((n_ctx,)),
            dma((n_ctx,)),
            dma((n_head, per_src)),
            dma((n_head, per_src)),
            dma((n_ctx,)),
            dma((n_ctx,)),
            dma((n_head,)),
            dma((n_head,)),
        ],
        compiler_params=pltpu.CompilerParams(
            collective_id=0, has_side_effects=True, vmem_limit_bytes=60 * 1024 * 1024
        ),
    )(block_pairs.T, pair_kinds.T, queries, out_grad, kv, log_sums, row_deltas)
    back = dkv.reshape(n_head, rows, 2 * width).transpose(1, 0, 2)
    return dq, back[:, :, :width], back[:, :, width:]


def solution(mesh):
    tokens = P(("ctx", "head"), None, None)
    stats = P("head", "ctx")
    return jax.shard_map(
        partial(shards, mesh.shape["ctx"], mesh.shape["head"]),
        mesh=mesh,
        in_specs=(tokens, tokens, tokens, tokens, stats, stats, P(), P()),
        out_specs=(tokens, tokens, tokens),
        check_vma=False,
    )
```

time: 160 us -> 56.4 us (0.35)
  Pallas kernels: 0 us -> 49.8 us
  waiting for transfers between devices: 48.3 us -> 0 us
  local copies, waits for them, and re-layouts: 45.9 us -> 3.74 us
  starting transfers between devices: 38.6 us -> 0 us
  matrix products: 13.4 us -> 0 us
  other arithmetic: 10.2 us -> 1.1 us
    pallas_call x0 -> x1, Pallas kernels: none -> 49.8 us  [shards(): pl.pallas_call(partial(kernel, n_ctx, n_head, n_slot), out_shape=(jax.Sha...]
    ppermute x6 -> x0, waiting for transfers between devices: 29.6 us -> none  [partner(): return lax.ppermute(block, axis, route)]
    all_to_all x7 -> x0, starting transfers between devices: 24.9 us -> none  [the longest x1 4.37 us: shards(): lax.all_to_all(key_states, 'head', split_axis=1, concat_axis=0, tiled=True)]
    all_to_all x7 -> x0, waiting for transfers between devices: 18.7 us -> none  [the longest x1 4.85 us: shards(): lax.all_to_all(query_out, 'head', split_axis=0, concat_axis=1, tiled=True)]
    gather x13 -> x0, local copies, waits for them, and re-layouts: 15.9 us -> none  [the longest x8 12.9 us: block_step(): tile_pair = kv_table[slot_index]]
    ppermute x6 -> x0, starting transfers between devices: 13.7 us -> none  [partner(): return lax.ppermute(block, axis, route)]
    dot_general x41 -> x0, matrix products: 13.4 us -> none  [the longest x8 3 us: tile_terms(): jnp.einsum(query_form + ',nkd->ngbk', query_part, key_tile, preferred_ele...]
    unnamed x28 -> x3, local copies, waits for them, and re-layouts: 11 us -> 0.97 us
  transfers between devices with their start and end apart: 13 -> 0, of which waited for: 13 -> 0; matrix products, arithmetic and copies ran while one was open for 10% -> 0% of each run, Pallas kernels for 0% -> 0%
where the time goes in v1:
time: 56.4 us; the launch traced here: 55.3 us
  Pallas kernels  49.8 us (88%)
  local copies, waits for them, and re-layouts  3.74 us (7%)
  other arithmetic  1.1 us (2%)
  between operations  0.65 us (1%)
    pallas_call x1, Pallas kernels, shards(): pl.pallas_call(partial(kernel, n_ctx, n_head, n_slot), out_shape=(jax.Sha...  49.8 us
    reshape x1, local copies, waits for them, and re-layouts, shards(): back = dkv.reshape(n_head, rows, 2 * width).transpose(1, 0, 2)  1.24 us

profile of v1, /device:TPU:0, one launch (start us, length us, event | category | flops | bytes accessed | tf_op | source)
XLA Modules:
  0.0 55.3 jit_solution(5766883575797671661)
XLA Ops:
  0.6 1.1 %maximum_bitcast_fusion = bf16[4,128,256]{2,0,1:T(4,128)(2,1)S(1)} fusion(bf16[128,4,128]{2,1,0:T(4,128)(2,1)} %param.10, bf16[128,4,128]{2,1,0:T(4,128)(2,1)} %param.9), kind=kLoop, calls=%fused_computation | loop fusion | flops 524288 | bytes 524288 | tf_op jit(solution)/shard_map/transpose | solution.py:377
  1.7 0.7 %copy.11 = bf16[4,128,256]{2,1,0:T(8,128)(2,1)} copy(bf16[4,128,256]{2,0,1:T(4,128)(2,1)S(1)} %maximum_bitcast_fusion) | data formatting | bytes 524288 | tf_op jit(solution)/shard_map/transpose | solution.py:377
  2.5 49.8 %shard_map.103 = (bf16[128,32,128]{2,1,0:T(8,128)(2,1)}, bf16[4,2,64,256]{3,2,1,0:T(8,128)(2,1)}) custom-call(s32[4,64]{1,0:T(4,128)} %bitcast.12, s32[4,64]{1,0:T(4,128)} %bitcast.13, bf16[128,32,128]{2,1,0:T(8,128)(2,1)} %q_hbm.1, bf16[128,32,128]{2,1,0:T(8,128)(2,1)} %g_hbm.1, bf16[4,2,64,256]{3,2,1,0:T(8,128)(2,1)} %bitcast.9, f32[8,512]{1,0:T(8,128)} %log_ref.1, ...), custom_call_target="tpu_custom_call" | custom-call | tf_op jit(solution)/shard_map/pallas_call | solution.py:382
  52.3 0.0 copy-start
  52.3 1.2 %copy.14 = bf16[4,128,256]{2,0,1:T(4,128)(2,1)S(1)} copy(bf16[4,128,256]{2,1,0:T(8,128)(2,1)} %bitcast.11) | data formatting | bytes 524288 | tf_op jit(solution)/shard_map/reshape | solution.py:433
  53.6 0.8 %fusion = (bf16[128,4,128]{2,1,0:T(4,128)(2,1)}, bf16[128,4,128]{2,1,0:T(4,128)(2,1)}) fusion(bf16[128,4,256]{2,1,0:T(4,128)(2,1)S(1)} %bitcast.10), kind=kLoop, calls=%fused_computation.2 | loop fusion | bytes 524288 | tf_op jit(solution)/shard_map/slice | solution.py:434
  54.4 0.0 copy-done
  54.4 1.0 %copy.16 = bf16[128,32,128]{2,1,0:T(8,128)(2,1)} copy(bf16[128,32,128]{2,1,0:T(8,128)(2,1)S(1)} %copy-done) | data formatting | bytes 2097152
Async XLA Ops:
  52.3 2.0 %copy-start = (bf16[128,32,128]{2,1,0:T(8,128)(2,1)S(1)}, bf16[128,32,128]{2,1,0:T(8,128)(2,1)}, u32[]{:S(2)}) copy-start(bf16[128,32,128]{2,1,0:T(8,128)(2,1)} %get-tuple-element.12) | copy-start | bytes 3145732

commit v2 on v1

--- a/solution.py
+++ b/solution.py
@@ -19,11 +19,13 @@
     kind_tab,
     q_hbm,
     g_hbm,
-    kv_in,
+    k_ref,
+    v_ref,
     log_ref,
     delta_ref,
     dq_out,
     dkv_out,
+    kv_in,
     q_buf,
     g_buf,
     kv_loc,
@@ -81,6 +83,12 @@
         return c
 
     lax.fori_loop(1, n_ctx, greet, 0)
+    for at, source in ((0, k_ref), (width, v_ref)):
+        whole = source[...].astype(jnp.float32)
+        for h in range(n_head):
+            kv_in[h, :, :, at : at + width] = (
+                whole[:, h].astype(jnp.bfloat16).reshape(per_src, BLOCK, width)
+            )
     pl.semaphore_wait(barrier, n_ctx + n_head - 2)
 
     def kv_copy(p):
@@ -215,8 +223,8 @@
         return jnp.where(kind_tab[j, at] > 0, lax.div(pair_tab[j, at], blocks), rank)
 
     def block_step(t, c):
-        d = t // per_src
-        j = lax.rem(t, per_src)
+        d = t // (2 * per_src) * 2 + lax.rem(t, 2)
+        j = lax.rem(t // 2, per_src)
         p = peer(d)
         i = p * per_src + j
         pltpu.make_async_copy(q_buf.at[p, j], q_buf.at[p, j], q_recv.at[p, j]).wait()
@@ -261,70 +269,72 @@
         def _():
             dq_copy(p, j).start()
 
-        acc[i + 1, :, :width] += dk[:BLOCK]
-        acc[i + 1, :, width:] += dv[:BLOCK]
-        acc[i, :, :width] += dk[BLOCK : 2 * BLOCK]
-        acc[i, :, width:] += dv[BLOCK : 2 * BLOCK]
-        acc_hub[:, :width] += dk[2 * BLOCK : 3 * BLOCK]
-        acc_hub[:, width:] += dv[2 * BLOCK : 3 * BLOCK]
-        for slot in range(3, n_slot):
-            far_terms[i, slot - 3, :, :width] = dk[slot * BLOCK : (slot + 1) * BLOCK]
-            far_terms[i, slot - 3, :, width:] = dv[slot * BLOCK : (slot + 1) * BLOCK]
+        for u, terms in enumerate((dk, dv)):
+            acc[u, i + 1] += terms[:BLOCK]
+            acc[u, i] += terms[BLOCK : 2 * BLOCK]
+            acc_hub[u] += terms[2 * BLOCK : 3 * BLOCK]
+            for slot in range(3, n_slot):
+                far_terms[u, i, slot - 3] = terms[slot * BLOCK : (slot + 1) * BLOCK]
         return c
 
     lax.fori_loop(0, blocks, block_step, 0)
 
-    def ret_copy(o):
-        return pltpu.make_async_remote_copy(
-            src_ref=part.at[o],
-            dst_ref=ret.at[rank],
-            send_sem=ret_send.at[o],
-            recv_sem=ret_recv.at[rank],
+    def ret_copy(u, o):
+        return pltpu.make_async_remote_copy(
+            src_ref=part.at[u, o],
+            dst_ref=ret.at[u, rank],
+            send_sem=ret_send.at[u, o],
+            recv_sem=ret_recv.at[u, rank],
             device_id=(o, me),
             device_id_type=MESH,
         )
 
-    def send_part(o, c):
-        terms = jnp.where(o == 0, acc_hub[...], 0.0) + jnp.where(o == rank - 1, acc[0], 0.0)
+    def send_part(u, o):
+        terms = jnp.where(o == 0, acc_hub[u], 0.0) + jnp.where(o == rank - 1, acc[u, 0], 0.0)
         for i in range(blocks):
             for slot in range(3, n_slot):
-                terms += jnp.where(far_owner(i, slot) == o, far_terms[i, slot - 3], 0.0)
-        part[o] = terms
-        ret_copy(o).start()
-        return c
-
-    lax.fori_loop(0, rank, send_part, 0)
-
-    acc[1] += jnp.where(rank == 0, acc_hub[...], 0.0)
-
-    def take_part(s, c):
-        pltpu.make_async_copy(ret.at[s], ret.at[s], ret_recv.at[s]).wait()
+                terms += jnp.where(far_owner(i, slot) == o, far_terms[u, i, slot - 3], 0.0)
+        part[u, o] = terms
+        ret_copy(u, o).start()
+
+    def take_part(u, s):
+        pltpu.make_async_copy(ret.at[u, s], ret.at[u, s], ret_recv.at[u, s]).wait()
         b = wanted_by(s)
         for i in range(blocks):
-            acc[i + 1] += jnp.where(b == i, ret[s], 0.0)
-        return c
-
-    lax.fori_loop(rank + 1, n_ctx, take_part, 0)
-
-    for i in range(blocks):
-        j = i % per_src
-        fin[i // per_src, j, :, :width] = (acc[i + 1, :, :width] * scale).astype(jnp.bfloat16)
-        fin[i // per_src, j, :, width:] = acc[i + 1, :, width:].astype(jnp.bfloat16)
-
-    def fin_copy(p):
-        return pltpu.make_async_remote_copy(
-            src_ref=fin.at[p],
-            dst_ref=dkv_out.at[me],
-            send_sem=fin_send.at[p],
-            recv_sem=fin_recv.at[me],
+            acc[u, i + 1] += jnp.where(b == i, ret[u, s], 0.0)
+
+    def fin_copy(u, p):
+        return pltpu.make_async_remote_copy(
+            src_ref=fin.at[u, p],
+            dst_ref=dkv_out.at[u, me],
+            send_sem=fin_send.at[u, p],
+            recv_sem=fin_recv.at[u, me],
             device_id=(rank, p),
             device_id_type=MESH,
         )
 
-    for d in far_first:
-        fin_copy(peer(d)).start()
-    own_fin = pltpu.make_async_copy(fin.at[me], dkv_out.at[me], fin_recv.at[me])
-    own_fin.start()
+    def own_fin(u):
+        return pltpu.make_async_copy(fin.at[u, me], dkv_out.at[u, me], fin_recv.at[u, me])
+
+    def each(step, u):
+        def body(k, c):
+            step(u, k)
+            return c
+
+        return body
+
+    for u in range(2):
+        lax.fori_loop(0, rank, each(send_part, u), 0)
+    for u in range(2):
+        acc[u, 1] += jnp.where(rank == 0, acc_hub[u], 0.0)
+        lax.fori_loop(rank + 1, n_ctx, each(take_part, u), 0)
+        for i in range(blocks):
+            fin[u, i // per_src, i % per_src] = (
+                acc[u, i + 1] * scale if u == 0 else acc[u, i + 1]
+            ).astype(jnp.bfloat16)
+        for d in far_first:
+            fin_copy(u, peer(d)).start()
+        own_fin(u).start()
 
     def sent_block(s, c):
         arr_copy(s).wait_send()
@@ -333,7 +343,8 @@
     lax.fori_loop(rank + 1, n_ctx, sent_block, 0)
 
     def sent_part(o, c):
-        ret_copy(o).wait_send()
+        ret_copy(0, o).wait_send()
+        ret_copy(1, o).wait_send()
         return c
 
     lax.fori_loop(0, rank, sent_part, 0)
@@ -348,11 +359,27 @@
                 pl.ds(j * BLOCK, BLOCK), pl.ds(pl.multiple_of(p * heads, heads), heads)
             ]
             pltpu.make_async_copy(dq_here, dq_here, dq_recv.at[p, j]).wait()
-        fin_copy(p).wait_send()
-        pltpu.make_async_copy(dkv_out.at[p], dkv_out.at[p], fin_recv.at[p]).wait()
+        for u in range(2):
+            fin_copy(u, p).wait_send()
+            fin_here = dkv_out.at[u, p]
+            pltpu.make_async_copy(fin_here, fin_here, fin_recv.at[u, p]).wait()
     for j in range(per_src):
         own_dq(j).wait()
-    own_fin.wait()
+    for u in range(2):
+        own_fin(u).wait()
+
+
+def tail(dq_in, dkv_in, dq_out, dk_out, dv_out, staged, sems):
+    load = pltpu.make_async_copy(dq_in, staged, sems.at[0])
+    load.start()
+    n_head, per_src, block, width = dkv_in.shape[1:]
+    for u, out in enumerate((dk_out, dv_out)):
+        by_head = dkv_in[u].astype(jnp.float32).reshape(n_head, per_src * block, width)
+        out[...] = jnp.stack([by_head[h] for h in range(n_head)], axis=1).astype(jnp.bfloat16)
+    load.wait()
+    store = pltpu.make_async_copy(staged, dq_out, sems.at[1])
+    store.start()
+    store.wait()
 
 
 def shards(
@@ -374,8 +401,7 @@
     blocks = per_src * n_head
     lanes = BLOCK * heads
     bf16, f32 = jnp.bfloat16, jnp.float32
-    kv = jnp.concatenate([key_states, value_states], axis=-1).transpose(1, 0, 2)
-    kv = kv.reshape(n_head, per_src, BLOCK, 2 * width)
+    half = (2, n_head, per_src, BLOCK, width)
     vmem = pl.BlockSpec(memory_space=pltpu.VMEM)
     anywhere = pl.BlockSpec(memory_space=pl.ANY)
     dma = pltpu.SemaphoreType.DMA
@@ -383,7 +409,7 @@
         partial(kernel, n_ctx, n_head, n_slot),
         out_shape=(
             jax.ShapeDtypeStruct(queries.shape, bf16),
-            jax.ShapeDtypeStruct(kv.shape, bf16),
+            jax.ShapeDtypeStruct(half, bf16),
         ),
         in_specs=[
             pl.BlockSpec(memory_space=pltpu.SMEM),
@@ -393,9 +419,11 @@
             vmem,
             vmem,
             vmem,
+            vmem,
         ],
         out_specs=(anywhere, vmem),
         scratch_shapes=[
+            pltpu.VMEM((n_head, per_src, BLOCK, 2 * width), bf16),
             pltpu.VMEM((n_head, per_src, BLOCK, heads, width), bf16),
             pltpu.VMEM((n_head, per_src, BLOCK, heads, width), bf16),
             pltpu.VMEM((blocks, BLOCK, 2 * width), bf16),
@@ -404,13 +432,13 @@
             pltpu.VMEM((n_slot * BLOCK, 2 * width), bf16),
             pltpu.VMEM((blocks, 1, lanes), f32),
             pltpu.VMEM((blocks, 1, lanes), f32),
-            pltpu.VMEM((blocks + 1, BLOCK, 2 * width), f32),
-            pltpu.VMEM((BLOCK, 2 * width), f32),
-            pltpu.VMEM((blocks, n_slot - 3, BLOCK, 2 * width), f32),
+            pltpu.VMEM((2, blocks + 1, BLOCK, width), f32),
+            pltpu.VMEM((2, BLOCK, width), f32),
+            pltpu.VMEM((2, blocks, n_slot - 3, BLOCK, width), f32),
             pltpu.VMEM((n_head, per_src, BLOCK, heads, width), bf16),
-            pltpu.VMEM((n_ctx, BLOCK, 2 * width), f32),
-            pltpu.VMEM((n_ctx, BLOCK, 2 * width), f32),
-            pltpu.VMEM((n_head, per_src, BLOCK, 2 * width), bf16),
+            pltpu.VMEM((2, n_ctx, BLOCK, width), f32),
+            pltpu.VMEM((2, n_ctx, BLOCK, width), f32),
+            pltpu.VMEM(half, bf16),
             dma((n_head,)),
             dma((n_head,)),
             dma((n_head, per_src)),
@@ -421,17 +449,26 @@
             dma((n_ctx,)),
             dma((n_head, per_src)),
             dma((n_head, per_src)),
-            dma((n_ctx,)),
-            dma((n_ctx,)),
-            dma((n_head,)),
-            dma((n_head,)),
+            dma((2, n_ctx)),
+            dma((2, n_ctx)),
+            dma((2, n_head)),
+            dma((2, n_head)),
         ],
         compiler_params=pltpu.CompilerParams(
             collective_id=0, has_side_effects=True, vmem_limit_bytes=60 * 1024 * 1024
         ),
-    )(block_pairs.T, pair_kinds.T, queries, out_grad, kv, log_sums, row_deltas)
-    back = dkv.reshape(n_head, rows, 2 * width).transpose(1, 0, 2)
-    return dq, back[:, :, :width], back[:, :, width:]
+    )(block_pairs.T, pair_kinds.T, queries, out_grad, key_states, value_states, log_sums, row_deltas)
+    return pl.pallas_call(
+        tail,
+        out_shape=(
+            jax.ShapeDtypeStruct(queries.shape, bf16),
+            jax.ShapeDtypeStruct(key_states.shape, bf16),
+            jax.ShapeDtypeStruct(value_states.shape, bf16),
+        ),
+        in_specs=[anywhere, vmem],
+        out_specs=(anywhere, vmem, vmem),
+        scratch_shapes=[pltpu.VMEM(queries.shape, bf16), dma((2,))],
+    )(dq, dkv)
 
 
 def solution(mesh):

time: 56.4 us -> 55.4 us (0.982); the launches traced: 55.3 us -> 55.2 us
  Pallas kernels: 49.8 us -> 54.5 us
  local copies, waits for them, and re-layouts: 3.74 us -> 0 us
  other arithmetic: 1.1 us -> 0 us
    pallas_call x0 -> x1, Pallas kernels: none -> 3.86 us  [shards(): pl.pallas_call(tail, out_shape=(jax.ShapeDtypeStruct(queries.shape, bf16)...]
    reshape x1 -> x0, local copies, waits for them, and re-layouts: 1.24 us -> none  [shards(): back = dkv.reshape(n_head, rows, 2 * width).transpose(1, 0, 2)]
    transpose x1 -> x0, other arithmetic: 1.1 us -> none  [shards(): kv = jnp.concatenate([key_states, value_states], axis=-1).transpose(1, 0, 2)]
    unnamed x3 -> x0, local copies, waits for them, and re-layouts: 0.97 us -> none
    pallas_call x1, Pallas kernels: 49.8 us -> 50.7 us  [shards(): pl.pallas_call(partial(kernel, n_ctx, n_head, n_slot), out_shape=(jax.Sha...]
    slice x1 -> x0, local copies, waits for them, and re-layouts: 0.79 us -> none  [shards(): return (dq, back[:, :, :width], back[:, :, width:])]
    transpose x1 -> x0, local copies, waits for them, and re-layouts: 0.73 us -> none  [shards(): kv = jnp.concatenate([key_states, value_states], axis=-1).transpose(1, 0, 2)]
where the time goes in v2:
time: 55.4 us; the launch traced here: 55.2 us
  Pallas kernels  54.5 us (98%)
  between operations  0.64 us (1%)
    pallas_call x1, Pallas kernels, shards(): pl.pallas_call(partial(kernel, n_ctx, n_head, n_slot), out_shape=(jax.Sha...  50.7 us
    pallas_call x1, Pallas kernels, shards(): pl.pallas_call(tail, out_shape=(jax.ShapeDtypeStruct(queries.shape, bf16)...  3.86 us

profile of v2, /device:TPU:0, one launch (start us, length us, event | category | flops | bytes accessed | tf_op | source)
XLA Modules:
  0.0 55.2 jit_solution(12614758258829642961)
XLA Ops:
  0.6 50.7 %shard_map.103 = (bf16[128,32,128]{2,1,0:T(8,128)(2,1)}, bf16[2,4,2,64,128]{4,3,2,1,0:T(8,128)(2,1)}) custom-call(s32[4,64]{1,0:T(4,128)} %bitcast.2, s32[4,64]{1,0:T(4,128)} %bitcast.3, bf16[128,32,128]{2,1,0:T(8,128)(2,1)} %q_hbm.1, bf16[128,32,128]{2,1,0:T(8,128)(2,1)} %g_hbm.1, bf16[128,4,128]{2,1,0:T(4,128)(2,1)} %k_ref.1, bf16[128,4,128]{2,1,0:T(4,128)(2,1)} %v_ref.1, ...), custom_call_target="tpu_custom_call" | custom-call | tf_op jit(solution)/shard_map/pallas_call | solution.py:408
  51.3 3.9 %shard_map.104 = (bf16[128,32,128]{2,1,0:T(8,128)(2,1)}, bf16[128,4,128]{2,1,0:T(4,128)(2,1)}, bf16[128,4,128]{2,1,0:T(4,128)(2,1)}) custom-call(bf16[128,32,128]{2,1,0:T(8,128)(2,1)} %get-tuple-element.5.dq_in, bf16[2,4,2,64,128]{4,3,2,1,0:T(8,128)(2,1)} %get-tuple-element.6.dkv_in), custom_call_target="tpu_custom_call" | custom-call | tf_op jit(solution)/shard_map/pallas_call | solution.py:461

commit v3 on v2

--- a/solution.py
+++ b/solution.py
@@ -24,7 +24,8 @@
     log_ref,
     delta_ref,
     dq_out,
-    dkv_out,
+    dk_out,
+    dv_land,
     kv_in,
     q_buf,
     g_buf,
@@ -41,6 +42,7 @@
     part,
     ret,
     fin,
+    dk_land,
     kv_send,
     kv_recv,
     q_send,
@@ -306,7 +308,7 @@
     def fin_copy(u, p):
         return pltpu.make_async_remote_copy(
             src_ref=fin.at[u, p],
-            dst_ref=dkv_out.at[u, me],
+            dst_ref=(dk_land, dv_land)[u].at[me],
             send_sem=fin_send.at[u, p],
             recv_sem=fin_recv.at[u, me],
             device_id=(rank, p),
@@ -314,7 +316,9 @@
         )
 
     def own_fin(u):
-        return pltpu.make_async_copy(fin.at[u, me], dkv_out.at[u, me], fin_recv.at[u, me])
+        return pltpu.make_async_copy(
+            fin.at[u, me], (dk_land, dv_land)[u].at[me], fin_recv.at[u, me]
+        )
 
     def each(step, u):
         def body(k, c):
@@ -335,6 +339,15 @@
         for d in far_first:
             fin_copy(u, peer(d)).start()
         own_fin(u).start()
+
+    def take_fin(u, land):
+        own_fin(u).wait()
+        for d in range(1, n_head):
+            p = peer(d)
+            pltpu.make_async_copy(land.at[p], land.at[p], fin_recv.at[u, p]).wait()
+
+    take_fin(0, dk_land)
+    dk_out[...] = by_token(dk_land)
 
     def sent_block(s, c):
         arr_copy(s).wait_send()
@@ -361,25 +374,31 @@
             pltpu.make_async_copy(dq_here, dq_here, dq_recv.at[p, j]).wait()
         for u in range(2):
             fin_copy(u, p).wait_send()
-            fin_here = dkv_out.at[u, p]
-            pltpu.make_async_copy(fin_here, fin_here, fin_recv.at[u, p]).wait()
     for j in range(per_src):
         own_dq(j).wait()
-    for u in range(2):
-        own_fin(u).wait()
-
-
-def tail(dq_in, dkv_in, dq_out, dk_out, dv_out, staged, sems):
-    load = pltpu.make_async_copy(dq_in, staged, sems.at[0])
-    load.start()
-    n_head, per_src, block, width = dkv_in.shape[1:]
-    for u, out in enumerate((dk_out, dv_out)):
-        by_head = dkv_in[u].astype(jnp.float32).reshape(n_head, per_src * block, width)
-        out[...] = jnp.stack([by_head[h] for h in range(n_head)], axis=1).astype(jnp.bfloat16)
-    load.wait()
-    store = pltpu.make_async_copy(staged, dq_out, sems.at[1])
-    store.start()
-    store.wait()
+    take_fin(1, dv_land)
+
+
+def by_token(land):
+    n_head, per_src, block, width = land.shape
+    heads = land[...].astype(jnp.float32).reshape(n_head, per_src * block, width)
+    return jnp.stack([heads[h] for h in range(n_head)], axis=1).astype(land.dtype)
+
+
+def tail(dq_in, dk_in, dv_in, dq_out, dk_out, dv_out, dq_held, dk_held, loads, stores):
+    pieces = loads.shape[0] - 1
+    step = dq_held.shape[0] // pieces
+    parts = [pl.ds(k * step, step) for k in range(pieces)]
+    routes = [(dq_in.at[at], dq_held.at[at], dq_out.at[at]) for at in parts]
+    routes.append((dk_in, dk_held, dk_out))
+    for k, (source, held, _) in enumerate(routes):
+        pltpu.make_async_copy(source, held, loads.at[k]).start()
+    for k, (source, held, target) in enumerate(routes):
+        pltpu.make_async_copy(source, held, loads.at[k]).wait()
+        pltpu.make_async_copy(held, target, stores.at[k]).start()
+    dv_out[...] = by_token(dv_in)
+    for k, (_, held, target) in enumerate(routes):
+        pltpu.make_async_copy(held, target, stores.at[k]).wait()
 
 
 def shards(
@@ -401,14 +420,15 @@
     blocks = per_src * n_head
     lanes = BLOCK * heads
     bf16, f32 = jnp.bfloat16, jnp.float32
-    half = (2, n_head, per_src, BLOCK, width)
+    half = (n_head, per_src, BLOCK, width)
     vmem = pl.BlockSpec(memory_space=pltpu.VMEM)
     anywhere = pl.BlockSpec(memory_space=pl.ANY)
     dma = pltpu.SemaphoreType.DMA
-    dq, dkv = pl.pallas_call(
+    dq, dk, dv = pl.pallas_call(
         partial(kernel, n_ctx, n_head, n_slot),
         out_shape=(
             jax.ShapeDtypeStruct(queries.shape, bf16),
+            jax.ShapeDtypeStruct(key_states.shape, bf16),
             jax.ShapeDtypeStruct(half, bf16),
         ),
         in_specs=[
@@ -421,7 +441,7 @@
             vmem,
             vmem,
         ],
-        out_specs=(anywhere, vmem),
+        out_specs=(anywhere, vmem, vmem),
         scratch_shapes=[
             pltpu.VMEM((n_head, per_src, BLOCK, 2 * width), bf16),
             pltpu.VMEM((n_head, per_src, BLOCK, heads, width), bf16),
@@ -438,6 +458,7 @@
             pltpu.VMEM((n_head, per_src, BLOCK, heads, width), bf16),
             pltpu.VMEM((2, n_ctx, BLOCK, width), f32),
             pltpu.VMEM((2, n_ctx, BLOCK, width), f32),
+            pltpu.VMEM((2,) + half, bf16),
             pltpu.VMEM(half, bf16),
             dma((n_head,)),
             dma((n_head,)),
@@ -465,10 +486,15 @@
             jax.ShapeDtypeStruct(key_states.shape, bf16),
             jax.ShapeDtypeStruct(value_states.shape, bf16),
         ),
-        in_specs=[anywhere, vmem],
-        out_specs=(anywhere, vmem, vmem),
-        scratch_shapes=[pltpu.VMEM(queries.shape, bf16), dma((2,))],
-    )(dq, dkv)
+        in_specs=[anywhere, anywhere, vmem],
+        out_specs=(anywhere, anywhere, vmem),
+        scratch_shapes=[
+            pltpu.VMEM(queries.shape, bf16),
+            pltpu.VMEM(key_states.shape, bf16),
+            dma((5,)),
+            dma((5,)),
+        ],
+    )(dq, dk, dv)
 
 
 def solution(mesh):

time: 55.4 us -> 55.1 us (level)
  no operation moved by 1% of the time
where the time goes in v3:
time: 55.1 us; the launch traced here: 54.9 us
  Pallas kernels  54.3 us (99%)
  between operations  0.64 us (1%)
    pallas_call x1, Pallas kernels, shards(): pl.pallas_call(partial(kernel, n_ctx, n_head, n_slot), out_shape=(jax.Sha...  50.7 us
    pallas_call x1, Pallas kernels, shards(): pl.pallas_call(tail, out_shape=(jax.ShapeDtypeStruct(queries.shape, bf16)...  3.59 us

profile of v3, /device:TPU:0, one launch (start us, length us, event | category | flops | bytes accessed | tf_op | source)
XLA Modules:
  0.0 54.9 jit_solution(3364510922500815401)
XLA Ops:
  0.6 50.7 %shard_map.103 = (bf16[128,32,128]{2,1,0:T(8,128)(2,1)}, bf16[128,4,128]{2,1,0:T(4,128)(2,1)}, bf16[4,2,64,128]{3,2,1,0:T(8,128)(2,1)}) custom-call(s32[4,64]{1,0:T(4,128)} %bitcast.2, s32[4,64]{1,0:T(4,128)} %bitcast.3, bf16[128,32,128]{2,1,0:T(8,128)(2,1)} %q_hbm.1, bf16[128,32,128]{2,1,0:T(8,128)(2,1)} %g_hbm.1, bf16[128,4,128]{2,1,0:T(4,128)(2,1)} %k_ref.1, ...), custom_call_target="tpu_custom_call" | custom-call | tf_op jit(solution)/shard_map/pallas_call | solution.py:427
  51.3 3.6 %shard_map.104 = (bf16[128,32,128]{2,1,0:T(8,128)(2,1)}, bf16[128,4,128]{2,1,0:T(4,128)(2,1)}, bf16[128,4,128]{2,1,0:T(4,128)(2,1)}) custom-call(bf16[128,32,128]{2,1,0:T(8,128)(2,1)} %get-tuple-element.6.dq_in, bf16[128,4,128]{2,1,0:T(4,128)(2,1)} %get-tuple-element.7.dk_in, bf16[4,2,64,128]{3,2,1,0:T(8,128)(2,1)} %get-tuple-element.8.dv_in), custom_call_target="tpu_custom_call" | custom-call | tf_op jit(solution)/shard_map/pallas_call | solution.py:482

commit v4 on v3

--- a/solution.py
+++ b/solution.py
@@ -26,6 +26,7 @@
     dq_out,
     dk_out,
     dv_land,
+    wide,
     kv_in,
     q_buf,
     g_buf,
@@ -86,10 +87,11 @@
 
     lax.fori_loop(1, n_ctx, greet, 0)
     for at, source in ((0, k_ref), (width, v_ref)):
-        whole = source[...].astype(jnp.float32)
+        wide[...] = source[...].astype(jnp.float32)
         for h in range(n_head):
-            kv_in[h, :, :, at : at + width] = (
-                whole[:, h].astype(jnp.bfloat16).reshape(per_src, BLOCK, width)
+            head_rows = wide[pl.ds(h, rows, stride=n_head), :]
+            kv_in[h, :, :, at : at + width] = head_rows.reshape(per_src, BLOCK, width).astype(
+                jnp.bfloat16
             )
     pl.semaphore_wait(barrier, n_ctx + n_head - 2)
 
@@ -144,13 +146,13 @@
     )
     for stat_ref, stat_rows in ((log_ref, log_rows), (delta_ref, delta_rows)):
         for i in range(blocks):
-            wide = jnp.dot(
+            by_lane = jnp.dot(
                 stat_ref[:, i * BLOCK : (i + 1) * BLOCK],
                 spread,
                 precision=lax.Precision.HIGHEST,
                 preferred_element_type=jnp.float32,
             )
-            stat_rows[i] = jnp.sum(jnp.where(own_row, wide, 0.0), axis=0, keepdims=True)
+            stat_rows[i] = jnp.sum(jnp.where(own_row, by_lane, 0.0), axis=0, keepdims=True)
     acc[...] = jnp.zeros_like(acc)
     acc_hub[...] = jnp.zeros_like(acc_hub)
 
@@ -347,7 +349,7 @@
             pltpu.make_async_copy(land.at[p], land.at[p], fin_recv.at[u, p]).wait()
 
     take_fin(0, dk_land)
-    dk_out[...] = by_token(dk_land)
+    dk_out[...] = by_token(dk_land, wide)
 
     def sent_block(s, c):
         arr_copy(s).wait_send()
@@ -379,13 +381,17 @@
     take_fin(1, dv_land)
 
 
-def by_token(land):
+def by_token(land, wide):
     n_head, per_src, block, width = land.shape
-    heads = land[...].astype(jnp.float32).reshape(n_head, per_src * block, width)
-    return jnp.stack([heads[h] for h in range(n_head)], axis=1).astype(land.dtype)
-
-
-def tail(dq_in, dk_in, dv_in, dq_out, dk_out, dv_out, dq_held, dk_held, loads, stores):
+    rows = per_src * block
+    for h in range(n_head):
+        wide[pl.ds(h, rows, stride=n_head), :] = (
+            land[h].astype(jnp.float32).reshape(rows, width)
+        )
+    return wide[...].astype(land.dtype)
+
+
+def tail(dq_in, dk_in, dv_in, dq_out, dk_out, dv_out, dq_held, dk_held, wide, loads, stores):
     pieces = loads.shape[0] - 1
     step = dq_held.shape[0] // pieces
     parts = [pl.ds(k * step, step) for k in range(pieces)]
@@ -396,7 +402,7 @@
     for k, (source, held, target) in enumerate(routes):
         pltpu.make_async_copy(source, held, loads.at[k]).wait()
         pltpu.make_async_copy(held, target, stores.at[k]).start()
-    dv_out[...] = by_token(dv_in)
+    dv_out[...] = by_token(dv_in, wide)
     for k, (_, held, target) in enumerate(routes):
         pltpu.make_async_copy(held, target, stores.at[k]).wait()
 
@@ -421,6 +427,7 @@
     lanes = BLOCK * heads
     bf16, f32 = jnp.bfloat16, jnp.float32
     half = (n_head, per_src, BLOCK, width)
+    flat = (rows * n_head, width)
     vmem = pl.BlockSpec(memory_space=pltpu.VMEM)
     anywhere = pl.BlockSpec(memory_space=pl.ANY)
     dma = pltpu.SemaphoreType.DMA
@@ -428,7 +435,7 @@
         partial(kernel, n_ctx, n_head, n_slot),
         out_shape=(
             jax.ShapeDtypeStruct(queries.shape, bf16),
-            jax.ShapeDtypeStruct(key_states.shape, bf16),
+            jax.ShapeDtypeStruct(flat, bf16),
             jax.ShapeDtypeStruct(half, bf16),
         ),
         in_specs=[
@@ -443,6 +450,7 @@
         ],
         out_specs=(anywhere, vmem, vmem),
         scratch_shapes=[
+            pltpu.VMEM(flat, f32),
             pltpu.VMEM((n_head, per_src, BLOCK, 2 * width), bf16),
             pltpu.VMEM((n_head, per_src, BLOCK, heads, width), bf16),
             pltpu.VMEM((n_head, per_src, BLOCK, heads, width), bf16),
@@ -478,23 +486,34 @@
         compiler_params=pltpu.CompilerParams(
             collective_id=0, has_side_effects=True, vmem_limit_bytes=60 * 1024 * 1024
         ),
-    )(block_pairs.T, pair_kinds.T, queries, out_grad, key_states, value_states, log_sums, row_deltas)
-    return pl.pallas_call(
+    )(
+        block_pairs.T,
+        pair_kinds.T,
+        queries,
+        out_grad,
+        key_states.reshape(flat),
+        value_states.reshape(flat),
+        log_sums,
+        row_deltas,
+    )
+    dq, dk, dv = pl.pallas_call(
         tail,
         out_shape=(
             jax.ShapeDtypeStruct(queries.shape, bf16),
-            jax.ShapeDtypeStruct(key_states.shape, bf16),
-            jax.ShapeDtypeStruct(value_states.shape, bf16),
+            jax.ShapeDtypeStruct(flat, bf16),
+            jax.ShapeDtypeStruct(flat, bf16),
         ),
         in_specs=[anywhere, anywhere, vmem],
         out_specs=(anywhere, anywhere, vmem),
         scratch_shapes=[
             pltpu.VMEM(queries.shape, bf16),
-            pltpu.VMEM(key_states.shape, bf16),
+            pltpu.VMEM(flat, bf16),
+            pltpu.VMEM(flat, f32),
             dma((5,)),
             dma((5,)),
         ],
     )(dq, dk, dv)
+    return dq, dk.reshape(key_states.shape), dv.reshape(value_states.shape)
 
 
 def solution(mesh):

time: 55.1 us -> 55.1 us (level)
  no operation moved by 1% of the time
where the time goes in v4:
time: 55.1 us; the launch traced here: 54.9 us
  Pallas kernels  54.3 us (99%)
  between operations  0.64 us (1%)
    pallas_call x1, Pallas kernels, shards(): pl.pallas_call(partial(kernel, n_ctx, n_head, n_slot), out_shape=(jax.Sha...  50.7 us
    pallas_call x1, Pallas kernels, shards(): pl.pallas_call(tail, out_shape=(jax.ShapeDtypeStruct(queries.shape, bf16)...  3.59 us

profile of v4, /device:TPU:0, one launch (start us, length us, event | category | flops | bytes accessed | tf_op | source)
XLA Modules:
  0.0 54.9 jit_solution(10550052657860520205)
XLA Ops:
  0.6 50.7 %shard_map.103 = (bf16[128,32,128]{2,1,0:T(8,128)(2,1)}, bf16[512,128]{1,0:T(8,128)(2,1)}, bf16[4,2,64,128]{3,2,1,0:T(8,128)(2,1)}) custom-call(s32[4,64]{1,0:T(4,128)} %bitcast.8, s32[4,64]{1,0:T(4,128)} %bitcast.9, bf16[128,32,128]{2,1,0:T(8,128)(2,1)} %q_hbm.1, bf16[128,32,128]{2,1,0:T(8,128)(2,1)} %g_hbm.1, bf16[512,128]{1,0:T(8,128)(2,1)} %bitcast.6, ...), custom_call_target="tpu_custom_call" | custom-call | tf_op jit(solution)/shard_map/pallas_call | solution.py:434
  51.3 3.6 %shard_map.104 = (bf16[128,32,128]{2,1,0:T(8,128)(2,1)}, bf16[512,128]{1,0:T(8,128)(2,1)}, bf16[512,128]{1,0:T(8,128)(2,1)}) custom-call(bf16[128,32,128]{2,1,0:T(8,128)(2,1)} %get-tuple-element.9.dq_in, bf16[512,128]{1,0:T(8,128)(2,1)} %get-tuple-element.10.dk_in, bf16[4,2,64,128]{3,2,1,0:T(8,128)(2,1)} %get-tuple-element.11.dv_in), custom_call_target="tpu_custom_call" | custom-call | tf_op jit(solution)/shard_map/pallas_call | solution.py:499

commit v5 on v4

--- a/solution.py
+++ b/solution.py
@@ -137,6 +137,42 @@
             token_copy(q_hbm, q_buf, q_send, q_recv, peer(d), j).start()
             token_copy(g_hbm, g_buf, g_send, g_recv, peer(d), j).start()
 
+    own_kv.wait()
+    for d in range(1, n_head):
+        p = peer(d)
+        kv_here = kv_loc.at[pl.ds(p * per_src, per_src)]
+        pltpu.make_async_copy(kv_here, kv_here, kv_recv.at[p]).wait()
+
+    first = rank * blocks
+
+    def wanted_by(s):
+        best = jnp.where(rank + 1 == s, blocks - 1, 0)
+        for i in range(blocks):
+            at = s * blocks + i
+            for j in range(3, n_slot):
+                local = pair_tab[j, at] - first
+                named = (kind_tab[j, at] > 0) & (local >= 0) & (local < blocks)
+                best = jnp.where(named, jnp.maximum(best, local), best)
+        return best
+
+    def arr_copy(s):
+        return pltpu.make_async_remote_copy(
+            src_ref=outgoing.at[s],
+            dst_ref=arrived.at[rank],
+            send_sem=arr_send.at[s],
+            recv_sem=arr_recv.at[rank],
+            device_id=(s, me),
+            device_id_type=MESH,
+        )
+
+    def send_block(s, c):
+        outgoing[s] = kv_loc[wanted_by(s)]
+        arr_copy(s).start()
+        return c
+
+    lax.fori_loop(rank + 1, n_ctx, send_block, 0)
+    arrived[rank] = kv_loc[0]
+
     spread = (
         lax.broadcasted_iota(jnp.int32, (BLOCK, lanes), 1) // heads
         == lax.broadcasted_iota(jnp.int32, (BLOCK, lanes), 0)
@@ -155,42 +191,6 @@
             stat_rows[i] = jnp.sum(jnp.where(own_row, by_lane, 0.0), axis=0, keepdims=True)
     acc[...] = jnp.zeros_like(acc)
     acc_hub[...] = jnp.zeros_like(acc_hub)
-
-    own_kv.wait()
-    for d in range(1, n_head):
-        p = peer(d)
-        kv_here = kv_loc.at[pl.ds(p * per_src, per_src)]
-        pltpu.make_async_copy(kv_here, kv_here, kv_recv.at[p]).wait()
-
-    first = rank * blocks
-
-    def wanted_by(s):
-        best = jnp.where(rank + 1 == s, blocks - 1, 0)
-        for i in range(blocks):
-            at = s * blocks + i
-            for j in range(3, n_slot):
-                local = pair_tab[j, at] - first
-                named = (kind_tab[j, at] > 0) & (local >= 0) & (local < blocks)
-                best = jnp.where(named, jnp.maximum(best, local), best)
-        return best
-
-    def arr_copy(s):
-        return pltpu.make_async_remote_copy(
-            src_ref=outgoing.at[s],
-            dst_ref=arrived.at[rank],
-            send_sem=arr_send.at[s],
-            recv_sem=arr_recv.at[rank],
-            device_id=(s, me),
-            device_id_type=MESH,
-        )
-
-    def send_block(s, c):
-        outgoing[s] = kv_loc[wanted_by(s)]
-        arr_copy(s).start()
-        return c
-
-    lax.fori_loop(rank + 1, n_ctx, send_block, 0)
-    arrived[rank] = kv_loc[0]
 
     def take_block(o, c):
         pltpu.make_async_copy(arrived.at[o], arrived.at[o], arr_recv.at[o]).wait()
@@ -391,20 +391,28 @@
     return wide[...].astype(land.dtype)
 
 
-def tail(dq_in, dk_in, dv_in, dq_out, dk_out, dv_out, dq_held, dk_held, wide, loads, stores):
-    pieces = loads.shape[0] - 1
+def tail(
+    dq_in, dk_in, dv_in, dq_out, dk_out, dv_out, dq_held, dk_held, dv_land, dv_held, wide, loads, stores
+):
+    pieces = loads.shape[0] - 2
     step = dq_held.shape[0] // pieces
     parts = [pl.ds(k * step, step) for k in range(pieces)]
+    load_dv = pltpu.make_async_copy(dv_in, dv_land, loads.at[pieces + 1])
+    store_dv = pltpu.make_async_copy(dv_held, dv_out, stores.at[pieces + 1])
     routes = [(dq_in.at[at], dq_held.at[at], dq_out.at[at]) for at in parts]
     routes.append((dk_in, dk_held, dk_out))
+    load_dv.start()
     for k, (source, held, _) in enumerate(routes):
         pltpu.make_async_copy(source, held, loads.at[k]).start()
+    load_dv.wait()
+    dv_held[...] = by_token(dv_land, wide)
+    store_dv.start()
     for k, (source, held, target) in enumerate(routes):
         pltpu.make_async_copy(source, held, loads.at[k]).wait()
         pltpu.make_async_copy(held, target, stores.at[k]).start()
-    dv_out[...] = by_token(dv_in, wide)
     for k, (_, held, target) in enumerate(routes):
         pltpu.make_async_copy(held, target, stores.at[k]).wait()
+    store_dv.wait()
 
 
 def shards(
@@ -503,14 +511,16 @@
             jax.ShapeDtypeStruct(flat, bf16),
             jax.ShapeDtypeStruct(flat, bf16),
         ),
-        in_specs=[anywhere, anywhere, vmem],
-        out_specs=(anywhere, anywhere, vmem),
+        in_specs=[anywhere] * 3,
+        out_specs=(anywhere,) * 3,
         scratch_shapes=[
             pltpu.VMEM(queries.shape, bf16),
             pltpu.VMEM(flat, bf16),
+            pltpu.VMEM(half, bf16),
+            pltpu.VMEM(flat, bf16),
             pltpu.VMEM(flat, f32),
-            dma((5,)),
-            dma((5,)),
+            dma((6,)),
+            dma((6,)),
         ],
     )(dq, dk, dv)
     return dq, dk.reshape(key_states.shape), dv.reshape(value_states.shape)

time: 55.1 us -> 53.6 us (0.973)
  Pallas kernels: 54.3 us -> 52.8 us
    pallas_call x1, Pallas kernels: 3.59 us -> 2.13 us  [shards(): pl.pallas_call(tail, out_shape=(jax.ShapeDtypeStruct(queries.shape, bf16)...]
where the time goes in v5:
time: 53.6 us; the launch traced here: 53.5 us
  Pallas kernels  52.8 us (99%)
  between operations  0.64 us (1%)
    pallas_call x1, Pallas kernels, shards(): pl.pallas_call(partial(kernel, n_ctx, n_head, n_slot), out_shape=(jax.Sha...  50.7 us
    pallas_call x1, Pallas kernels, shards(): pl.pallas_call(tail, out_shape=(jax.ShapeDtypeStruct(queries.shape, bf16)...  2.13 us

profile of v5, /device:TPU:0, one launch (start us, length us, event | category | flops | bytes accessed | tf_op | source)
XLA Modules:
  0.0 53.5 jit_solution(11325774480827360199)
XLA Ops:
  0.6 50.7 %shard_map.103 = (bf16[128,32,128]{2,1,0:T(8,128)(2,1)}, bf16[512,128]{1,0:T(8,128)(2,1)}, bf16[4,2,64,128]{3,2,1,0:T(8,128)(2,1)}) custom-call(s32[4,64]{1,0:T(4,128)} %bitcast.8, s32[4,64]{1,0:T(4,128)} %bitcast.9, bf16[128,32,128]{2,1,0:T(8,128)(2,1)} %q_hbm.1, bf16[128,32,128]{2,1,0:T(8,128)(2,1)} %g_hbm.1, bf16[512,128]{1,0:T(8,128)(2,1)} %bitcast.6, ...), custom_call_target="tpu_custom_call" | custom-call | tf_op jit(solution)/shard_map/pallas_call | solution.py:442
  51.3 2.1 %shard_map.104 = (bf16[128,32,128]{2,1,0:T(8,128)(2,1)}, bf16[512,128]{1,0:T(8,128)(2,1)}, bf16[512,128]{1,0:T(8,128)(2,1)}) custom-call(bf16[128,32,128]{2,1,0:T(8,128)(2,1)} %get-tuple-element.9.dq_in, bf16[512,128]{1,0:T(8,128)(2,1)} %get-tuple-element.10.dk_in, bf16[4,2,64,128]{3,2,1,0:T(8,128)(2,1)} %get-tuple-element.11.dv_in), custom_call_target="tpu_custom_call" | custom-call | tf_op jit(solution)/shard_map/pallas_call | solution.py:507
